TPU v7x, 512 devices: a whole 4x4x16 slice. The times are simulated.
512 devices in a mesh: space: 32 (over z, core), tm: 16 (over y, x).
Axes of the slice: x: 4, y: 4, z: 16, core: 2. Of those that a mesh axis runs over, the one named last changes fastest.
Arguments:
- snapshots: bfloat16 [65536, 16384], P('space', 'tm'), may hold values from -6 to 6
- basis: bfloat16 [65536, 256], P(('space', 'tm')), may hold values from -0.0234375 to 0.0234375
- lengths: int32 [16, 64], P('tm'), may hold values from 1 to 61, as said below
- owners: int32 [16, 64], P('tm'), may hold values from 0 to 31, as said below
Outputs:
- gram_out: bfloat16 [16, 32, 392, 392], P('tm', 'space')
- target_out: bfloat16 [16, 32, 392, 256], P('tm', 'space')
Inputs may be any that keep to these rules, and one draw needn't show every extreme that they name: Each row of lengths sums to 1024. The trajectories that one owner holds in one row have 62 snapshots together at most, and in every row some owner holds exactly 62. `owners`: in every row each space index owns exactly two trajectories.
All inputs are finite; a program needn't handle non-finite values.
Results may differ from a plain program's by a relative error of at most 0.0057.
Values may be sent and summed in bfloat16 or wider, within the bound.
No kernel may reach another device: no remote copies, remote signals or barrier semaphores. Data moves between devices by JAX's collectives and lax.ppermute only.
A program may use at most 64 MiB of HBM per device.

v0:
```python
import jax
import jax.numpy as jnp
import numpy as np
from jax import lax
from jax.sharding import PartitionSpec as P

QM = 16


def slot_plan(length_row, owner_row, owner_count, capacity, snap_count):
    traj_end = jnp.cumsum(length_row)
    starts = traj_end - length_row
    snap_index = jnp.arange(snap_count, dtype=jnp.int32)
    member = (
        (snap_index[:, None] >= starts[None, :]) & (snap_index[:, None] < traj_end[None, :])
    ).astype(jnp.int32)
    snap_start = jnp.sum(member * starts[None, :], axis=1)
    snap_end = jnp.sum(member * traj_end[None, :], axis=1)
    snap_owner = jnp.sum(member * owner_row[None, :], axis=1)
    traj_index = jnp.arange(length_row.shape[0], dtype=jnp.int32)
    same_owner = owner_row[:, None] == owner_row[None, :]
    earlier = traj_index[None, :] < traj_index[:, None]
    offset = jnp.sum(jnp.where(same_owner & earlier, length_row[None, :], 0), axis=1)
    slot_index = jnp.sum(member * offset[None, :], axis=1) + snap_index - snap_start
    has_next = (snap_index + 1 < snap_end).astype(jnp.int32)
    destination = snap_owner * capacity + slot_index
    source_rows = jnp.full((owner_count * capacity,), -1, jnp.int32).at[destination].set(snap_index)
    live_rows = jnp.zeros((owner_count * capacity,), jnp.int32).at[destination].set(has_next)
    return (source_rows, live_rows)


def library(coords, live_slots, weight_scale):
    first_mode, second_mode = np.triu_indices(QM)
    products = coords[:, first_mode] * coords[:, second_mode]
    library_rows = jnp.concatenate([coords, products], axis=1).astype(jnp.bfloat16)
    successor = jnp.concatenate(
        [coords[1:], jnp.zeros((1, coords.shape[1]), jnp.float32)], axis=0
    ).astype(jnp.bfloat16)
    weighted = library_rows * live_slots[:, None].astype(jnp.bfloat16)
    dims = (((0,), (0,)), ((), ()))
    gram_matrix = (
        lax.dot_general(weighted, library_rows, dims, preferred_element_type=jnp.float32)
        * weight_scale
    )
    targets = (
        lax.dot_general(weighted, successor, dims, preferred_element_type=jnp.float32)
        * weight_scale
    )
    return (gram_matrix.astype(jnp.bfloat16), targets.astype(jnp.bfloat16))


def on_device(snapshots, basis, lengths, owners):
    dims = (((0,), (0,)), ((), ()))
    snap_count = snapshots.shape[1]
    gathered = lax.all_gather(basis, "tm", axis=0, tiled=True)
    partial_value = lax.dot_general(snapshots, gathered, dims, preferred_element_type=jnp.float32)
    owner_count = lax.axis_size("space")
    capacity = 2 * snap_count // owner_count - 2
    source_rows, live_rows = slot_plan(lengths[0], owners[0], owner_count, capacity, snap_count)
    own_index = lax.axis_index("space")
    mine = lax.dynamic_slice_in_dim(source_rows, own_index * capacity, capacity)
    summed = lax.psum(partial_value, "space")
    packed = jnp.take(summed, jnp.maximum(mine, 0), axis=0) * (mine >= 0)[:, None].astype(
        jnp.float32
    )
    live_slots = lax.dynamic_slice_in_dim(live_rows, own_index * capacity, capacity)
    gram_matrix, targets = library(packed, live_slots, owner_count / snap_count)
    return (gram_matrix[None, None], targets[None, None])


def solution(mesh):
    placed = (P("space", "tm"), P(("space", "tm"), None), P("tm", None), P("tm", None))
    return jax.shard_map(
        on_device,
        mesh=mesh,
        in_specs=placed,
        out_specs=(P("tm", "space", None, None), P("tm", "space", None, None)),
        check_vma=False,
    )
```

profile of v0, /device:TPU:1, one launch (start us, length us, event | category | flops | bytes accessed | tf_op | source)
XLA Modules:
  0.0 301.7 jit_solution(7914927873324652971)
XLA Ops:
  7.2 0.7 all-gather.2.cloned.1.call-update
  7.9 0.0 all-reduce.3.cloned.1.call-start
  7.9 0.7 copy.20
  8.7 0.1 reduce-window.4
  8.8 0.1 reduce
  8.9 0.9 select_reduce_fusion.4
  9.8 0.7 fusion.17
  10.5 0.8 select_reduce_fusion
  11.4 4.3 %scatter_custom_fusion.1 = s32[1984]{0:T(1024)S(1)} fusion(s32[1024]{0:T(1024)S(1)} %bitcast.28, s32[1024]{0:T(1024)S(1)} %fusion.16, s32[]{:T(128)} %constant.22.clone.1), kind=kCustom, calls=%fused_computation.35 | custom fusion | bytes 7940 | tf_op jit(solution)/shard_map/scatter | solution.py:28
  15.7 4.3 %scatter_custom_fusion = s32[1984]{0:T(1024)S(1)} fusion(s32[1024]{0:T(1024)S(1)} %bitcast.29, s32[1024]{0:T(1024)S(1)} %iota.19, s32[]{:T(128)} %constant.21.clone.1), kind=kCustom, calls=%fused_computation.37 | custom fusion | bytes 7940 | tf_op jit(solution)/shard_map/scatter | solution.py:27
  20.1 52.9 %all-gather.2.cloned.1.call-done = bf16[2048,256]{1,0:T(8,128)(2,1)} async-done(((bf16[128,256]{1,0:T(8,128)(2,1)}), bf16[2048,256]{1,0:T(8,128)(2,1)}) %all-gather.2.cloned.1.call-update) | async-done | bytes 1048592 | tf_op jit(solution)/shard_map/all_gather | solution.py:55
  72.9 4.8 %fusion.22 = f32[1024,256]{1,0:T(8,128)} fusion(bf16[2048,1024]{1,0:T(8,128)(2,1)} %param.8, bf16[2048,256]{1,0:T(8,128)(2,1)} %all-gather.2.cloned.1.call-done), kind=kOutput, calls=%fused_computation.51 | convolution fusion | flops 1073741824 | bytes 6291456 | tf_op jit(solution)/shard_map/dot_general | solution.py:56
  77.7 0.1 dynamic-slice_convert_fusion
  77.8 0.1 broadcast_compare_fusion
  77.9 211.2 %all-reduce.3.cloned.1.call-done = f32[1024,256]{1,0:T(8,128)} async-done(((f32[1024,256]{1,0:T(8,128)}), f32[1024,256]{1,0:T(8,128)}) %all-reduce.3.cloned.1.call-update) | async-done | bytes 1048592 | tf_op jit(solution)/shard_map/psum | solution.py:62
  289.2 1.9 gather_fusion
  291.0 0.1 fusion.21
  291.1 0.1 copy.21
  291.2 0.7 gather_fusion.2
  291.9 0.7 gather_fusion.1
  292.6 0.1 copy.23
  292.7 0.1 copy.24
  292.8 1.1 fusion.1
  293.9 1.0 fusion.3
  (15 shorter events, 0.1 us)
Async XLA Ops:
  7.2 65.8 %all-gather.2.cloned.1.call-start = ((), (), s32[]{:S(2)}) async-start(), calls=%async_computation | async-start | bytes 1114112 | tf_op jit(solution)/shard_map/all_gather | solution.py:55
  7.9 281.3 %all-reduce.3.cloned.1.call-start = ((), (), s32[]{:S(2)}) async-start(), calls=%async_computation.1 | async-start | bytes 2097152 | tf_op jit(solution)/shard_map/psum | solution.py:62
  20.0 57.8 %copy-start.1 = (s32[136]{0:T(256)S(1)}, s32[136]{0:T(256)}, u32[]{:S(2)}) copy-start(s32[136]{0:T(256)} %constant.68) | copy-start | bytes 1636
  20.1 57.8 %copy-start = (s32[136]{0:T(256)S(1)}, s32[136]{0:T(256)}, u32[]{:S(2)}) copy-start(s32[136]{0:T(256)} %constant.69) | copy-start | bytes 1636
Sparse Core Ops, SparseCore 0:
  11.0 61.8 all-gather.1
  77.8 211.2 all-reduce.2
where the time goes:
time: 302 us
  waiting for transfers between devices  265 us (88%)
  between operations  14.2 us (5%)
  local copies, waits for them, and re-layouts  12.9 us (4%)
  matrix products  6.86 us (2%)
    psum x1, waiting for transfers between devices, on_device(): summed = lax.psum(partial_value, 'space')  211 us
    all_gather x1, waiting for transfers between devices, on_device(): gathered = lax.all_gather(basis, 'tm', axis=0, tiled=True)  52.9 us
  transfers between devices with their start and end apart: 2, of which 2 were waited for; matrix products, arithmetic and copies ran while one was open for 4% of the time, Pallas kernels for 0%

commit v1 on v0

--- a/solution.py
+++ b/solution.py
@@ -52,7 +52,8 @@
 def on_device(snapshots, basis, lengths, owners):
     dims = (((0,), (0,)), ((), ()))
     snap_count = snapshots.shape[1]
-    gathered = lax.all_gather(basis, "tm", axis=0, tiled=True)
+    sent = jnp.stack([basis] * lax.axis_size("tm"))
+    gathered = jnp.concatenate(lax.all_to_all(sent, "tm", 0, 0), axis=0)
     partial_value = lax.dot_general(snapshots, gathered, dims, preferred_element_type=jnp.float32)
     owner_count = lax.axis_size("space")
     capacity = 2 * snap_count // owner_count - 2

time: 302 us -> 263 us (0.87)
  waiting for transfers between devices: 265 us -> 216 us
  starting transfers between devices: 0.08 us -> 7.63 us
    all_gather x1 -> x0, waiting for transfers between devices: 52.9 us -> none  [on_device(): gathered = lax.all_gather(basis, 'tm', axis=0, tiled=True)]
    all_to_all x0 -> x1, starting transfers between devices: none -> 7.58 us  [on_device(): gathered = jnp.concatenate(lax.all_to_all(sent, 'tm', 0, 0), axis=0)]
  transfers between devices with their start and end apart: 2 -> 2, of which waited for: 2 -> 2; matrix products, arithmetic and copies ran while one was open for 4% -> 5% of each run, Pallas kernels for 0% -> 0%
where the time goes in v1:
time: 263 us
  waiting for transfers between devices  216 us (82%)
  local copies, waits for them, and re-layouts  14.8 us (6%)
  between operations  14.2 us (5%)
  starting transfers between devices  7.63 us (3%)
  matrix products  6.63 us (3%)
  other arithmetic  2.93 us (1%)
    psum x1, waiting for transfers between devices, on_device(): summed = lax.psum(partial_value, 'space')  214 us
    all_to_all x1, starting transfers between devices, on_device(): gathered = jnp.concatenate(lax.all_to_all(sent, 'tm', 0, 0), axis=0)  7.58 us
  transfers between devices with their start and end apart: 2, of which 2 were waited for; matrix products, arithmetic and copies ran while one was open for 5% of the time, Pallas kernels for 0%

profile of v1, /device:TPU:1, one launch (start us, length us, event | category | flops | bytes accessed | tf_op | source)
XLA Modules:
  0.0 262.6 jit_solution(4654364162013349227)
XLA Ops:
  7.2 1.9 stack.2
  9.1 7.6 %all-to-all-start = ((bf16[16,128,256]{2,1,0:T(8,128)(2,1)}), bf16[16,128,256]{2,1,0:T(8,128)(2,1)S(1)}, u32[]{:S(2)}, u32[]{:S(2)}) async-start(bf16[16,128,256]{2,1,0:T(8,128)(2,1)} %stack.2), calls=%async_computation | async-start | bytes 2097152 | tf_op jit(solution)/shard_map/all_to_all | solution.py:56
  16.7 0.7 copy.20
  17.5 0.1 reduce-window.4
  17.6 0.1 reduce
  17.7 0.9 select_reduce_fusion.4
  18.6 0.7 fusion.17
  19.3 0.8 select_reduce_fusion
  20.2 4.3 %scatter_custom_fusion.1 = s32[1984]{0:T(1024)S(1)} fusion(s32[1024]{0:T(1024)S(1)} %bitcast.28, s32[1024]{0:T(1024)S(1)} %fusion.16, s32[]{:T(128)} %constant.22.clone.1), kind=kCustom, calls=%fused_computation.35 | custom fusion | bytes 7940 | tf_op jit(solution)/shard_map/scatter | solution.py:28
  24.5 4.3 %scatter_custom_fusion = s32[1984]{0:T(1024)S(1)} fusion(s32[1024]{0:T(1024)S(1)} %bitcast.29, s32[1024]{0:T(1024)S(1)} %iota.19, s32[]{:T(128)} %constant.21.clone.1), kind=kCustom, calls=%fused_computation.37 | custom fusion | bytes 7940 | tf_op jit(solution)/shard_map/scatter | solution.py:27
  28.8 2.3 all-to-all-done
  31.2 4.5 %fusion.22 = f32[1024,256]{1,0:T(8,128)} fusion(bf16[2048,1024]{1,0:T(8,128)(2,1)} %param.8, bf16[2048,256]{1,0:T(8,128)(2,1)S(1)} %bitcast.22), kind=kOutput, calls=%fused_computation.51 | convolution fusion | flops 1073741824 | bytes 6291456 | tf_op jit(solution)/shard_map/dot_general | solution.py:57
  35.7 0.1 dynamic-slice_convert_fusion
  35.8 0.1 broadcast_compare_fusion
  35.9 214.1 %all-reduce.3.cloned.1.call-done = f32[1024,256]{1,0:T(8,128)} async-done(((f32[1024,256]{1,0:T(8,128)}), f32[1024,256]{1,0:T(8,128)}) %all-reduce.3.cloned.1.call-update) | async-done | bytes 1048592 | tf_op jit(solution)/shard_map/psum | solution.py:63
  250.0 1.9 gather_fusion
  251.9 0.1 fusion.21
  252.0 0.1 copy.21
  252.1 0.7 gather_fusion.1
  252.8 0.1 copy.23
  252.9 0.7 gather_fusion.2
  253.5 0.1 copy.24
  253.7 1.1 fusion.1
  254.8 1.0 fusion.3
  (15 shorter events, 0.1 us)
Async XLA Ops:
  9.1 22.1 %all-to-all-start = ((bf16[16,128,256]{2,1,0:T(8,128)(2,1)}), bf16[16,128,256]{2,1,0:T(8,128)(2,1)S(1)}, u32[]{:S(2)}, u32[]{:S(2)}) async-start(bf16[16,128,256]{2,1,0:T(8,128)(2,1)} %stack.2), calls=%async_computation | async-start | bytes 2097152 | tf_op jit(solution)/shard_map/all_to_all | solution.py:56
  16.7 233.3 %all-reduce.3.cloned.1.call-start = ((), (), s32[]{:S(2)}) async-start(), calls=%async_computation.1 | async-start | bytes 2097152 | tf_op jit(solution)/shard_map/psum | solution.py:63
  31.2 4.7 %copy-start.1 = (s32[136]{0:T(256)S(1)}, s32[136]{0:T(256)}, u32[]{:S(2)}) copy-start(s32[136]{0:T(256)} %constant.68) | copy-start | bytes 1636
  31.2 4.8 %copy-start = (s32[136]{0:T(256)S(1)}, s32[136]{0:T(256)}, u32[]{:S(2)}) copy-start(s32[136]{0:T(256)} %constant.69) | copy-start | bytes 1636
Sparse Core Ops, SparseCore 0:
  35.8 214.1 all-reduce.2
